TPU v7x, 256 devices: a whole 4x4x8 slice. The times are simulated.
256 devices in a mesh: seq: 32 (over x, y, core), dp: 8 (over z).
Axes of the slice: x: 4, y: 4, z: 8, core: 2. Of those that a mesh axis runs over, the one named last changes fastest.
Arguments:
- queries: bfloat16 [8, 16384, 2048], P('dp', 'seq'), may hold values from -5 to 5
- keys: bfloat16 [8, 16384, 2048], P('dp', 'seq'), may hold values from -5 to 5
- values: bfloat16 [8, 16384, 2048], P('dp', 'seq'), may hold values from -8 to 8
- out_weight: bfloat16 [2048, 4096], P(None, 'dp'), may hold values from -0.125 to 0.125
Outputs:
- projected: bfloat16 [8, 16384, 4096], P('dp', 'seq')
All inputs are finite; a program needn't handle non-finite values.
Results may differ from a plain program's by a relative error of at most 0.0061.
Values may be sent and summed in bfloat16 or wider, within the bound.
No kernel may reach another device: no remote copies, remote signals or barrier semaphores. Data moves between devices by JAX's collectives and lax.ppermute only.
A program may use at most 192 MiB of HBM per device.

v0:
```python
import math
import jax
import jax.numpy as jnp
from jax import lax
from jax.sharding import PartitionSpec as P

CHANNEL_WIDTH = 128
SEGMENT_LENGTH = 256


def prefix(value, axis, join, neutral):
    count, mine = (lax.axis_size(axis), lax.axis_index(axis))
    pieces = jax.tree.map(lambda part: lax.all_gather(part, axis), value)
    subtotal = jax.tree.map(
        lambda part, zero: jnp.full_like(part, 0) + jnp.asarray(zero, part.dtype), value, neutral
    )

    def turn(position, subtotal):
        longer = join(subtotal, jax.tree.map(lambda part: part[position], pieces))
        return jax.tree.map(lambda new, old: jnp.where(position < mine, new, old), longer, subtotal)

    return lax.fori_loop(0, count - 1, turn, subtotal)


def shifted(block, axis, distance):
    devices = range(lax.axis_size(axis))
    route = [(i - distance, i) for i in devices if i - distance in devices]
    return lax.ppermute(block, axis, route)


def add_pair(earlier_pair, later_pair):
    return (earlier_pair[0] + later_pair[0], earlier_pair[1] + later_pair[1])


def per_device(queries, keys, values, out_weight):
    local_rows = queries.shape[1]
    feature_width = queries.shape[2]
    head_count = feature_width // CHANNEL_WIDTH
    local_blocks = local_rows // SEGMENT_LENGTH
    shard_count = lax.axis_size("seq")
    shard_index = lax.axis_index("seq")
    total_blocks = local_blocks * shard_count
    first_block = shard_index * local_blocks
    softmax_multiplier = 1.0 / math.sqrt(CHANNEL_WIDTH)
    faraway_offset_bias = math.log(SEGMENT_LENGTH)
    own_queries = queries[0]
    own_keys = keys[0]
    own_values = values[0]
    span_address_means = jnp.mean(
        own_keys.reshape(local_blocks, SEGMENT_LENGTH, feature_width), axis=1, dtype=jnp.float32
    ).astype(jnp.bfloat16)
    value_means = jnp.mean(
        own_values.reshape(local_blocks, SEGMENT_LENGTH, feature_width), axis=1, dtype=jnp.float32
    ).astype(jnp.bfloat16)
    empty_buffer = jnp.zeros((total_blocks, feature_width), jnp.bfloat16)
    slot_keys = lax.dynamic_update_slice_in_dim(empty_buffer, span_address_means, first_block, 0)
    slot_values = lax.dynamic_update_slice_in_dim(empty_buffer, value_means, first_block, 0)
    far_keys, far_values = prefix(
        (slot_keys, slot_values), "seq", add_pair, (empty_buffer, empty_buffer)
    )
    prev_keys, prev_values = shifted(
        (own_keys[local_rows - SEGMENT_LENGTH :], own_values[local_rows - SEGMENT_LENGTH :]),
        "seq",
        1,
    )
    near_keys = jnp.concatenate([prev_keys, own_keys], axis=0)
    near_values = jnp.concatenate([prev_values, own_values], axis=0)
    far_k = far_keys.reshape(total_blocks, head_count, CHANNEL_WIDTH)
    far_v = far_values.reshape(total_blocks, head_count, CHANNEL_WIDTH)
    far_index = jnp.arange(total_blocks, dtype=jnp.int32)
    group_rows = SEGMENT_LENGTH * math.gcd(local_blocks, max(1, 512 // SEGMENT_LENGTH))
    request_vectors = own_queries.reshape(group_rows, head_count, CHANNEL_WIDTH)
    address_vectors = near_keys.reshape(group_rows + SEGMENT_LENGTH, head_count, CHANNEL_WIDTH)
    value_rows = near_values.reshape(group_rows + SEGMENT_LENGTH, head_count, CHANNEL_WIDTH)
    query_local = 0 + jnp.arange(group_rows, dtype=jnp.int32)
    key_local = 0 - SEGMENT_LENGTH + jnp.arange(group_rows + SEGMENT_LENGTH, dtype=jnp.int32)
    query_blk = query_local // SEGMENT_LENGTH
    key_blk = key_local // SEGMENT_LENGTH
    within_block = (key_blk[None, :] == query_blk[:, None]) & (
        key_local[None, :] <= query_local[:, None]
    )
    preceding_segment = (key_blk[None, :] == query_blk[:, None] - 1) & (
        (key_blk[None, :] >= 0) | (shard_index > 0)
    )
    adjacent_similarity = (
        jnp.einsum(
            "qhd,khd->hqk", request_vectors, address_vectors, preferred_element_type=jnp.float32
        )
        * softmax_multiplier
    )
    adjacent_similarity = jnp.where(
        (within_block | preceding_segment)[None], adjacent_similarity, -jnp.inf
    )
    query_global = first_block + query_blk
    faraway_similarity = (
        jnp.einsum("qhd,jhd->hqj", request_vectors, far_k, preferred_element_type=jnp.float32)
        * softmax_multiplier
        + faraway_offset_bias
    )
    faraway_similarity = jnp.where(
        (far_index[None, :] < query_global[:, None] - 1)[None], faraway_similarity, -jnp.inf
    )
    row_max = jnp.maximum(
        jnp.max(adjacent_similarity, axis=-1), jnp.max(faraway_similarity, axis=-1)
    )[..., None]
    near_w = jnp.exp(adjacent_similarity - row_max)
    far_w = jnp.exp(faraway_similarity - row_max)
    row_total = jnp.sum(near_w, axis=-1, keepdims=True) + jnp.sum(far_w, axis=-1, keepdims=True)
    near_p = (near_w / row_total).astype(jnp.bfloat16)
    far_p = (far_w / row_total).astype(jnp.bfloat16)
    attended = jnp.einsum("hqk,khd->qhd", near_p, value_rows, preferred_element_type=jnp.float32)
    attended = attended + jnp.einsum(
        "hqj,jhd->qhd", far_p, far_v, preferred_element_type=jnp.float32
    )
    pieces = attended.astype(jnp.bfloat16).reshape(group_rows, feature_width)
    projected = jnp.dot(
        pieces,
        lax.all_gather(out_weight, "dp", axis=1, tiled=True),
        preferred_element_type=jnp.float32,
    ).astype(jnp.bfloat16)
    return projected[None]


def solution(mesh):
    return jax.shard_map(
        per_device,
        mesh=mesh,
        in_specs=(P("dp", "seq", None), P("dp", "seq", None), P("dp", "seq", None), P(None, "dp")),
        out_specs=P("dp", "seq", None),
        check_vma=False,
    )
```

profile of v0, /device:TPU:1, one launch (start us, length us, event | category | flops | bytes accessed | tf_op | source)
XLA Modules:
  0.0 340.8 jit_solution(379502660158891560)
XLA Ops:
  6.5 2.1 convert_reduce_fusion.1
  11.4 3.9 %copy.25 = bf16[1,512,2048]{1,2,0:T(8,128)(2,1)} copy(bf16[1,512,2048]{2,1,0:T(8,128)(2,1)} %param.7) | data formatting | bytes 4194304 | tf_op args[1]
  15.4 2.3 slice_bitcast_fusion
  17.7 4.6 %collective-permute-start.1 = (bf16[256,2048]{0,1:T(8,128)(2,1)}, bf16[256,2048]{0,1:T(8,128)(2,1)}, u32[]{:S(2)}, u32[]{:S(2)}) collective-permute-start(bf16[256,2048]{0,1:T(8,128)(2,1)} %slice_bitcast_fusion), channel_id=1, source_target_pairs={{0,8},{8,16},{16,24},{24,32},{32,40},{40,48},{48,56},{56,64},{64,7... | collective-permute-start | bytes 3145736 | tf_op jit(solution)/shard_map/ppermute | solution.py:28
  23.3 1.9 collective-permute-start
  25.2 2.5 copy.24
  27.7 3.7 %copy.37 = bf16[64,8,16,128]{3,2,1,0:T(8,128)(2,1)} copy(bf16[64,8,16,128]{3,1,2,0:T(8,128)(2,1)} %bitcast.68) | data formatting | bytes 4194304
  31.4 2.4 copy.28
  34.7 3.3 collective-permute-done.1
  38.1 2.3 copy.27
  40.3 9.4 %collective-permute-done = bf16[256,2048]{1,0:T(8,128)(2,1)} collective-permute-done((bf16[256,2048]{1,0:T(8,128)(2,1)}, bf16[256,2048]{1,0:T(8,128)(2,1)}, u32[]{:S(2)}, u32[]{:S(2)}) %collective-permute-start) | collective-permute-done | bytes 1048608 | tf_op jit(solution)/shard_map/ppermute | solution.py:28
  49.7 2.3 copy.23
  52.0 12.3 %fusion.1 = (f32[16,512]{1,0:T(8,128)S(1)}, f32[16,768,512]{2,1,0:T(8,128)}) fusion(pred[512,768]{0,1:T(8,128)(4,1)S(1)} %fusion.20, bf16[512,16,128]{2,1,0:T(8,128)(2,1)S(1)} %bitcast.70, bf16[512,16,128]{2,0,1:T(8,128)(2,1)} %copy.28, bf16[256,16,128]{2,0,1:T(8,128)(2,1)} %copy.27), kind=kOutput, calls=%fused_computation.6 | convolution fusion | flops 1635770368 | bytes 30834688 | tf_op jit(solution)/shard_map/qhd,khd->hqk/dot_general | solution.py:86
  64.3 21.8 %all-gather.4.cloned.1.call-done = bf16[32,64,2048]{2,1,0:T(8,128)(2,1)} async-done(((bf16[1,64,2048]{2,1,0:T(8,128)(2,1)}), bf16[32,64,2048]{2,1,0:T(8,128)(2,1)}) %all-gather.4.cloned.1.call-update) | async-done | bytes 8388624 | tf_op jit(solution)/shard_map/all_gather | solution.py:13
  86.1 60.0 %all-gather.6.cloned.1.call-done = bf16[32,64,2048]{2,1,0:T(8,128)(2,1)} async-done(((bf16[1,64,2048]{2,1,0:T(8,128)(2,1)}), bf16[32,64,2048]{2,1,0:T(8,128)(2,1)}) %all-gather.6.cloned.1.call-update) | async-done | bytes 8388624 | tf_op jit(solution)/shard_map/all_gather | solution.py:13
  146.2 39.2 %while.16 = (s32[]{:T(128)}, bf16[64,2048]{1,0:T(8,128)(2,1)S(1)}, bf16[64,2048]{1,0:T(8,128)(2,1)S(1)}, s32[]{:T(128)}, bf16[32,64,2048]{2,1,0:T(8,128)(2,1)}, ...) while((s32[]{:T(128)}, bf16[64,2048]{1,0:T(8,128)(2,1)S(1)}, ...), condition=%wide.region_4.5_spmd.clone, body=%wide.region_3.4_spmd.clone.sunk | while | flops 786436 | bytes 1572973 | solution.py:22
  147.4 1.2 add_select_fusion.5
  148.7 1.2 add_select_fusion.5
  149.9 1.2 add_select_fusion.5
  151.2 1.2 add_select_fusion.5
  152.5 1.2 add_select_fusion.5
  155.0 1.2 add_select_fusion.5
  156.2 1.2 add_select_fusion.5
  158.8 1.3 add_select_fusion.5
  160.1 1.3 add_select_fusion.5
  161.4 1.2 add_select_fusion.5
  163.9 1.2 add_select_fusion.5
  165.2 1.2 add_select_fusion.5
  166.4 1.2 add_select_fusion.5
  167.7 1.2 add_select_fusion.5
  168.9 1.2 add_select_fusion.5
  170.2 1.2 add_select_fusion.5
  171.5 1.2 add_select_fusion.5
  172.7 1.2 add_select_fusion.5
  174.0 1.2 add_select_fusion.5
  175.3 1.2 add_select_fusion.5
  176.5 1.2 add_select_fusion.5
  177.8 1.2 add_select_fusion.5
  179.1 1.2 add_select_fusion.5
  180.3 1.2 add_select_fusion.5
  181.6 1.2 add_select_fusion.5
  182.9 1.2 add_select_fusion.5
  185.4 1.5 fusion.42
  187.3 11.3 %fusion = f32[16,512]{1,0:T(8,128)S(1)} fusion(f32[16,768,512]{2,1,0:T(8,128)} %get-tuple-element.153, f32[16,512]{1,0:T(8,128)S(1)} %max.7, pred[512,768]{0,1:T(8,128)(4,1)S(1)} %fusion.20), kind=kLoop, calls=%fused_computation.5 | loop fusion | flops 25157632 | bytes 25624576 | tf_op jit(solution)/shard_map/reduce_sum | solution.py:108
  198.5 2.8 fusion.21
  201.3 14.6 %add_convert_fusion = bf16[16,128,512]{2,1,0:T(8,128)(2,1)} fusion(f32[16,128,512]{2,1,0:T(8,128)} %fusion.21, f32[16,768,512]{2,1,0:T(8,128)} %get-tuple-element.153, f32[16,512]{1,0:T(8,128)S(1)} %add.130, f32[16,512]{1,0:T(8,128)S(1)} %max.7, pred[512,768]{0,1:T(8,128)(4,1)S(1)} %fusion.20, bf16[512,16,128]{0,2,1:T(8,128)(2,1)S(1)} %bitcast.69, ...), kind=kOutput, calls=%fused_computation.12 | convolution fusion | flops 1650458624 | bytes 35061760 | tf_op jit(solution)/shard_map/hqk,khd->qhd/dot_general | solution.py:111
  215.9 103.9 %all-gather.8.cloned.1.call-done = bf16[2048,4096]{1,0:T(8,128)(2,1)} async-done(((bf16[2048,512]{1,0:T(8,128)(2,1)}), bf16[2048,4096]{1,0:T(8,128)(2,1)}) %all-gather.8.cloned.1.call-update) | async-done | bytes 16777232 | tf_op jit(solution)/shard_map/all_gather | solution.py:118
  319.8 14.5 %fusion.3 = bf16[1,512,4096]{2,1,0:T(8,128)(2,1)} fusion(bf16[512,2048]{0,1:T(8,128)(2,1)} %bitcast.73, bf16[2048,4096]{1,0:T(8,128)(2,1)} %all-gather.8.cloned.1.call-done), kind=kOutput, calls=%fused_computation.9 | convolution fusion | flops 8592031744 | bytes 23068672 | tf_op jit(solution)/shard_map/dot_general | solution.py:116
  (40 shorter events, 11.2 us)
Async XLA Ops:
  6.5 3.0 copy-start
  6.5 79.6 %all-gather.4.cloned.1.call-start = ((), (), s32[]{:S(2)}) async-start(), calls=%async_computation | async-start | bytes 8650752 | tf_op jit(solution)/shard_map/all_gather | solution.py:13
  8.7 0.7 copy-start.5
  9.5 136.7 %all-gather.6.cloned.1.call-start = ((), (), s32[]{:S(2)}) async-start(), calls=%async_computation.1 | async-start | bytes 8650752 | tf_op jit(solution)/shard_map/all_gather | solution.py:13
  10.0 0.7 copy-start.4
  10.7 309.1 %all-gather.8.cloned.1.call-start = ((), (), s32[]{:S(2)}) async-start(), calls=%async_computation.2 | async-start | bytes 18874368 | tf_op jit(solution)/shard_map/all_gather | solution.py:118
  17.7 20.4 %collective-permute-start.1 = (bf16[256,2048]{0,1:T(8,128)(2,1)}, bf16[256,2048]{0,1:T(8,128)(2,1)}, u32[]{:S(2)}, u32[]{:S(2)}) collective-permute-start(bf16[256,2048]{0,1:T(8,128)(2,1)} %slice_bitcast_fusion), channel_id=1, source_target_pairs={{0,8},{8,16},{16,24},{24,32},{32,40},{40,48},{48,56},{56,64},{64,7... | collective-permute-start | bytes 3145736 | tf_op jit(solution)/shard_map/ppermute | solution.py:28
  23.3 26.4 %collective-permute-start = (bf16[256,2048]{1,0:T(8,128)(2,1)}, bf16[256,2048]{1,0:T(8,128)(2,1)}, u32[]{:S(2)}, u32[]{:S(2)}) collective-permute-start(bf16[256,2048]{1,0:T(8,128)(2,1)} %slice_bitcast_fusion.1), channel_id=1, source_target_pairs={{0,8},{8,16},{16,24},{24,32},{32,40},{40,48},{48,56},{56,64},{64,7... | collective-permute-start | bytes 3145736 | tf_op jit(solution)/shard_map/ppermute | solution.py:28
  27.7 3.7 %copy-start.1 = (bf16[1,512,2048]{1,2,0:T(8,128)(2,1)S(1)}, bf16[1,512,2048]{1,2,0:T(8,128)(2,1)}, u32[]{:S(2)}) copy-start(bf16[1,512,2048]{1,2,0:T(8,128)(2,1)} %copy.25) | copy-start | bytes 6291460
  33.8 18.2 %copy-start.3 = (bf16[64,8,16,128]{3,2,1,0:T(8,128)(2,1)S(1)}, bf16[64,8,16,128]{3,2,1,0:T(8,128)(2,1)}, u32[]{:S(2)}) copy-start(bf16[64,8,16,128]{3,2,1,0:T(8,128)(2,1)} %copy.37) | copy-start | bytes 6291460
  198.5 2.8 copy-start.2
Sparse Core Ops, SparseCore 0:
  9.9 76.2 all-gather.3
  88.7 57.4 all-gather.5
  148.0 171.7 all-gather.7
where the time goes:
time: 342 us; the launch traced here: 341 us
  waiting for transfers between devices  199 us (58%)
  other arithmetic  53.6 us (16%)
  matrix products  45.6 us (13%)
  local copies, waits for them, and re-layouts  21.8 us (6%)
  between operations  13.3 us (4%)
  starting transfers between devices  6.57 us (2%)
    all_gather x1, waiting for transfers between devices, per_device(): lax.all_gather(out_weight, 'dp', axis=1, tiled=True)  104 us
    all_gather x2, waiting for transfers between devices, prefix(): pieces = jax.tree.map(lambda part: lax.all_gather(part, axis), value)  81.8 us
    select_n x31, other arithmetic, turn(): jnp.where(position < mine, new, old)  38.5 us
    dot_general x1, matrix products, per_device(): jnp.einsum('hqk,khd->qhd', near_p, value_rows, preferred_element_type=jnp...  14.6 us
    dot_general x1, matrix products, per_device(): jnp.dot(pieces, lax.all_gather(out_weight, 'dp', axis=1, tiled=True), pre...  14.5 us
    ppermute x2, waiting for transfers between devices, shifted(): return lax.ppermute(block, axis, route)  12.7 us
    dot_general x1, matrix products, per_device(): jnp.einsum('qhd,khd->hqk', request_vectors, address_vectors, preferred_el...  12.3 us
    unnamed x15, local copies, waits for them, and re-layouts  11.5 us
  transfers between devices with their start and end apart: 5, of which 5 were waited for; matrix products, arithmetic and copies ran while one was open for 30% of the time, Pallas kernels for 0%

commit v1 on v0

--- a/solution.py
+++ b/solution.py
@@ -115,7 +115,9 @@
     pieces = attended.astype(jnp.bfloat16).reshape(group_rows, feature_width)
     projected = jnp.dot(
         pieces,
-        lax.all_gather(out_weight, "dp", axis=1, tiled=True),
+        jnp.concatenate(
+            lax.all_to_all(jnp.stack([out_weight] * lax.axis_size("dp")), "dp", 0, 0), axis=1
+        ),
         preferred_element_type=jnp.float32,
     ).astype(jnp.bfloat16)
     return projected[None]

time: 342 us -> 420 us (1.23)
  waiting for transfers between devices: 199 us -> 258 us
  local copies, waits for them, and re-layouts: 21.8 us -> 32.7 us
  starting transfers between devices: 6.57 us -> 15.2 us
    all_to_all x0 -> x1, waiting for transfers between devices: none -> 189 us  [per_device(): lax.all_to_all(jnp.stack([out_weight] * lax.axis_size('dp')), 'dp', 0, 0)]
    all_gather x1 -> x0, waiting for transfers between devices: 104 us -> none  [per_device(): lax.all_gather(out_weight, 'dp', axis=1, tiled=True)]
    all_gather x2, waiting for transfers between devices: 81.8 us -> 44.3 us  [prefix(): pieces = jax.tree.map(lambda part: lax.all_gather(part, axis), value)]
    ppermute x2, waiting for transfers between devices: 12.7 us -> 25.1 us  [shifted(): return lax.ppermute(block, axis, route)]
    all_to_all x0 -> x1, starting transfers between devices: none -> 9 us  [per_device(): lax.all_to_all(jnp.stack([out_weight] * lax.axis_size('dp')), 'dp', 0, 0)]
    another operation x0 -> x1, local copies, waits for them, and re-layouts: none -> 6.87 us  [per_device(): jnp.stack([out_weight] * lax.axis_size('dp'))]
    unnamed x15 -> x16, local copies, waits for them, and re-layouts: 11.5 us -> 15.5 us
  transfers between devices with their start and end apart: 5 -> 5, of which waited for: 5 -> 4; matrix products, arithmetic and copies ran while one was open for 30% -> 27% of each run, Pallas kernels for 0% -> 0%
where the time goes in v1:
time: 420 us; the launch traced here: 419 us
  waiting for transfers between devices  258 us (61%)
  other arithmetic  53.3 us (13%)
  matrix products  45.3 us (11%)
  local copies, waits for them, and re-layouts  32.7 us (8%)
  starting transfers between devices  15.2 us (4%)
  between operations  13.6 us (3%)
    all_to_all x1, waiting for transfers between devices, per_device(): lax.all_to_all(jnp.stack([out_weight] * lax.axis_size('dp')), 'dp', 0, 0)  189 us
    all_gather x2, waiting for transfers between devices, prefix(): pieces = jax.tree.map(lambda part: lax.all_gather(part, axis), value)  44.3 us
    select_n x31, other arithmetic, turn(): jnp.where(position < mine, new, old)  38.3 us
    ppermute x2, waiting for transfers between devices, shifted(): return lax.ppermute(block, axis, route)  25.1 us
    unnamed x16, local copies, waits for them, and re-layouts  15.5 us
    dot_general x1, matrix products, per_device(): jnp.dot(pieces, jnp.concatenate(lax.all_to_all(jnp.stack([out_weight] * l...  14.4 us
    dot_general x1, matrix products, per_device(): jnp.einsum('hqk,khd->qhd', near_p, value_rows, preferred_element_type=jnp...  14.3 us
    dot_general x1, matrix products, per_device(): jnp.einsum('qhd,khd->hqk', request_vectors, address_vectors, preferred_el...  12.4 us
  transfers between devices with their start and end apart: 5, of which 4 were waited for; matrix products, arithmetic and copies ran while one was open for 27% of the time, Pallas kernels for 0%

profile of v1, /device:TPU:1, one launch (start us, length us, event | category | flops | bytes accessed | tf_op | source)
XLA Modules:
  0.0 419.0 jit_solution(14634214453570480860)
XLA Ops:
  6.5 2.1 convert_reduce_fusion.1
  10.7 3.9 copy.35
  14.6 6.9 %stack.2 = bf16[8,2048,512]{1,2,0:T(8,128)(2,1)} broadcast(bf16[2048,512]{0,1:T(8,128)(2,1)} %copy.35), dimensions={1,2} | broadcast | bytes 18874368 | tf_op jit(solution)/shard_map/stack | solution.py:119
  21.5 9.0 %all-to-all-start = ((bf16[8,2048,512]{1,2,0:T(8,128)(2,1)}), bf16[8,2048,512]{1,2,0:T(8,128)(2,1)}, u32[]{:S(2)}, u32[]{:S(2)}) async-start(bf16[8,2048,512]{1,2,0:T(8,128)(2,1)} %stack.2), calls=%async_computation | async-start | bytes 33554432 | tf_op jit(solution)/shard_map/all_to_all | solution.py:119
  30.5 3.9 copy.26
  34.4 2.3 slice_bitcast_fusion
  36.7 4.0 collective-permute-start.1
  41.8 2.1 collective-permute-start
  43.9 2.5 copy.25
  46.5 3.7 copy.39
  50.2 2.4 copy.29
  53.5 4.9 %collective-permute-done.1 = bf16[256,2048]{0,1:T(8,128)(2,1)} collective-permute-done((bf16[256,2048]{0,1:T(8,128)(2,1)}, bf16[256,2048]{0,1:T(8,128)(2,1)}, u32[]{:S(2)}, u32[]{:S(2)}) %collective-permute-start.1) | collective-permute-done | bytes 1048608 | tf_op jit(solution)/shard_map/ppermute | solution.py:28
  58.4 2.2 copy.28
  60.6 20.3 %collective-permute-done = bf16[256,2048]{1,0:T(8,128)(2,1)} collective-permute-done((bf16[256,2048]{1,0:T(8,128)(2,1)}, bf16[256,2048]{1,0:T(8,128)(2,1)}, u32[]{:S(2)}, u32[]{:S(2)}) %collective-permute-start) | collective-permute-done | bytes 1048608 | tf_op jit(solution)/shard_map/ppermute | solution.py:28
  80.9 2.3 copy.24
  83.2 12.4 %fusion.1 = (f32[16,512]{1,0:T(8,128)S(1)}, f32[16,768,512]{2,1,0:T(8,128)}) fusion(pred[512,768]{0,1:T(8,128)(4,1)S(1)} %fusion.20, bf16[512,16,128]{2,1,0:T(8,128)(2,1)S(1)} %bitcast.73, bf16[512,16,128]{2,0,1:T(8,128)(2,1)} %copy.29, bf16[256,16,128]{2,0,1:T(8,128)(2,1)} %copy.28), kind=kOutput, calls=%fused_computation.6 | convolution fusion | flops 1635770368 | bytes 30834688 | tf_op jit(solution)/shard_map/qhd,khd->hqk/dot_general | solution.py:86
  95.6 44.3 %all-gather.5.cloned.1.call-done = bf16[32,64,2048]{2,1,0:T(8,128)(2,1)} async-done(((bf16[1,64,2048]{2,1,0:T(8,128)(2,1)}), bf16[32,64,2048]{2,1,0:T(8,128)(2,1)}) %all-gather.5.cloned.1.call-update) | async-done | bytes 8388624 | tf_op jit(solution)/shard_map/all_gather | solution.py:13
  139.9 39.1 %while.16 = (s32[]{:T(128)}, bf16[64,2048]{1,0:T(8,128)(2,1)S(1)}, bf16[64,2048]{1,0:T(8,128)(2,1)S(1)}, s32[]{:T(128)}, bf16[32,64,2048]{2,1,0:T(8,128)(2,1)}, ...) while((s32[]{:T(128)}, bf16[64,2048]{1,0:T(8,128)(2,1)S(1)}, ...), condition=%wide.region_4.5_spmd.clone, body=%wide.region_3.4_spmd.clone.sunk | while | flops 786436 | bytes 1572973 | solution.py:22
  141.1 1.2 add_select_fusion.5
  142.4 1.2 add_select_fusion.5
  143.6 1.2 add_select_fusion.5
  144.9 1.2 add_select_fusion.5
  146.2 1.2 add_select_fusion.5
  147.4 1.2 add_select_fusion.5
  149.9 1.2 add_select_fusion.5
  151.2 1.2 add_select_fusion.5
  153.7 1.2 add_select_fusion.5
  155.0 1.2 add_select_fusion.5
  157.5 1.2 add_select_fusion.5
  158.8 1.2 add_select_fusion.5
  160.0 1.2 add_select_fusion.5
  161.3 1.2 add_select_fusion.5
  162.5 1.2 add_select_fusion.5
  163.8 1.2 add_select_fusion.5
  165.1 1.2 add_select_fusion.5
  166.3 1.2 add_select_fusion.5
  167.6 1.2 add_select_fusion.5
  170.1 1.2 add_select_fusion.5
  171.4 1.2 add_select_fusion.5
  173.9 1.2 add_select_fusion.5
  175.2 1.2 add_select_fusion.5
  177.7 1.2 add_select_fusion.5
  178.9 1.5 fusion.42
  180.8 11.1 %fusion = f32[16,512]{1,0:T(8,128)S(1)} fusion(f32[16,768,512]{2,1,0:T(8,128)} %get-tuple-element.153, f32[16,512]{1,0:T(8,128)S(1)} %max.7, pred[512,768]{0,1:T(8,128)(4,1)S(1)} %fusion.20), kind=kLoop, calls=%fused_computation.5 | loop fusion | flops 25157632 | bytes 25624576 | tf_op jit(solution)/shard_map/reduce_sum | solution.py:108
  192.0 2.8 fusion.21
  194.7 14.3 %add_convert_fusion = bf16[16,128,512]{2,1,0:T(8,128)(2,1)} fusion(f32[16,128,512]{2,1,0:T(8,128)} %fusion.21, f32[16,768,512]{2,1,0:T(8,128)} %get-tuple-element.153, f32[16,512]{1,0:T(8,128)S(1)} %add.130, f32[16,512]{1,0:T(8,128)S(1)} %max.7, pred[512,768]{0,1:T(8,128)(4,1)S(1)} %fusion.20, bf16[512,16,128]{0,2,1:T(8,128)(2,1)S(1)} %bitcast.72, ...), kind=kOutput, calls=%fused_computation.12 | convolution fusion | flops 1650458624 | bytes 35061760 | tf_op jit(solution)/shard_map/hqk,khd->qhd/dot_general | solution.py:111
  209.0 188.7 %all-to-all-done = bf16[8,2048,512]{1,2,0:T(8,128)(2,1)} async-done(((bf16[8,2048,512]{1,2,0:T(8,128)(2,1)}), bf16[8,2048,512]{1,2,0:T(8,128)(2,1)}, u32[]{:S(2)}, u32[]{:S(2)}) %all-to-all-start) | async-done | bytes 16777248 | tf_op jit(solution)/shard_map/all_to_all | solution.py:119
  397.7 14.4 %fusion.3 = bf16[1,512,4096]{2,1,0:T(8,128)(2,1)} fusion(bf16[512,2048]{0,1:T(8,128)(2,1)} %bitcast.76, bf16[2048,4096]{0,1:T(8,128)(2,1)} %bitcast.15), kind=kOutput, calls=%fused_computation.9 | convolution fusion | flops 8592031744 | bytes 23068672 | tf_op jit(solution)/shard_map/dot_general | solution.py:116
  (41 shorter events, 12.9 us)
Async XLA Ops:
  6.5 3.0 copy-start
  6.5 89.1 %all-gather.3.cloned.1.call-start = ((), (), s32[]{:S(2)}) async-start(), calls=%async_computation.1 | async-start | bytes 8650752 | tf_op jit(solution)/shard_map/all_gather | solution.py:13
  8.7 0.7 copy-start.5
  9.5 130.4 %all-gather.5.cloned.1.call-start = ((), (), s32[]{:S(2)}) async-start(), calls=%async_computation.2 | async-start | bytes 8650752 | tf_op jit(solution)/shard_map/all_gather | solution.py:13
  10.0 0.7 copy-start.4
  21.5 376.2 %all-to-all-start = ((bf16[8,2048,512]{1,2,0:T(8,128)(2,1)}), bf16[8,2048,512]{1,2,0:T(8,128)(2,1)}, u32[]{:S(2)}, u32[]{:S(2)}) async-start(bf16[8,2048,512]{1,2,0:T(8,128)(2,1)} %stack.2), calls=%async_computation | async-start | bytes 33554432 | tf_op jit(solution)/shard_map/all_to_all | solution.py:119
  36.7 21.6 %collective-permute-start.1 = (bf16[256,2048]{0,1:T(8,128)(2,1)}, bf16[256,2048]{0,1:T(8,128)(2,1)}, u32[]{:S(2)}, u32[]{:S(2)}) collective-permute-start(bf16[256,2048]{0,1:T(8,128)(2,1)} %slice_bitcast_fusion), channel_id=1, source_target_pairs={{0,8},{8,16},{16,24},{24,32},{32,40},{40,48},{48,56},{56,64},{64,7... | collective-permute-start | bytes 3145736 | tf_op jit(solution)/shard_map/ppermute | solution.py:28
  41.8 39.1 %collective-permute-start = (bf16[256,2048]{1,0:T(8,128)(2,1)}, bf16[256,2048]{1,0:T(8,128)(2,1)}, u32[]{:S(2)}, u32[]{:S(2)}) collective-permute-start(bf16[256,2048]{1,0:T(8,128)(2,1)} %slice_bitcast_fusion.1), channel_id=1, source_target_pairs={{0,8},{8,16},{16,24},{24,32},{32,40},{40,48},{48,56},{56,64},{64,7... | collective-permute-start | bytes 3145736 | tf_op jit(solution)/shard_map/ppermute | solution.py:28
  46.5 3.7 copy-start.1
  52.6 30.6 %copy-start.3 = (bf16[64,8,16,128]{3,2,1,0:T(8,128)(2,1)S(1)}, bf16[64,8,16,128]{3,2,1,0:T(8,128)(2,1)}, u32[]{:S(2)}) copy-start(bf16[64,8,16,128]{3,2,1,0:T(8,128)(2,1)} %copy.39) | copy-start | bytes 6291460
  191.9 2.8 copy-start.2
Sparse Core Ops, SparseCore 0:
  9.9 67.5 all-gather.2
  80.0 59.7 all-gather.4
